TPU v7x, 32 devices: a whole 2x2x4 slice. The times are simulated.
32 devices in a mesh: scen: 2 (over y), dw: 4 (over x, core), reg: 4 (over z).
Axes of the slice: x: 2, y: 2, z: 4, core: 2. Of those that a mesh axis runs over, the one named last changes fastest.
Arguments:
- load_base: float32 [96, 65536], P(None, ('scen', 'dw', 'reg')), parts along dimension 1, may hold values from -24 to 24
- kkt_inverse: float32 [64, 96, 96], replicated, may hold values from -1 to 2
- archetype: int32 [65536], P(('scen', 'dw', 'reg')), parts along dimension 0, may hold values from 0 to 63
- feeder: int32 [65536], P(('scen', 'dw', 'reg')), parts along dimension 0, may hold values from 0 to 255, as said below
- live_counts: int32 [32, 4], P(('scen', 'dw', 'reg')), parts along dimension 0, may hold values from 1 to 512, as said below
- feeder_cap: int32 [512], P(('scen', 'dw', 'reg')), parts along dimension 0, may hold values from 1000 to 11999
- dual_start: float32 [512, 96], P(('scen', 'dw', 'reg')), parts along dimension 0, may hold values from 0 to 1
- balance_target: float32 [192], P('scen'), parts along dimension 0, may hold values from -6 to 6
Outputs:
- roster: float32 [96, 65536], P(None, ('scen', 'dw', 'reg')), parts along dimension 1
- feeder_duals: float32 [512, 96], P(('scen', 'dw', 'reg')), parts along dimension 0
- balance_dual: float32 [192], P('scen'), parts along dimension 0
There are 2 independent parts, one for each index of `scen`. A program takes and returns all parts, laid end to end along the dimension named above; an argument that names none is the same for every part. Nothing has to cross between parts.
Inputs may be any that keep to these rules, and one draw needn't show every extreme that they name: The feeder of the dwelling in slot s of the device at index j along dw and r along reg lies in block k * 4 + r of 16 feeders, where k = s // 512. `live_counts`: row d (devices in the order dw+reg) gives for each block k the number of leading slots of that block that hold a dwelling; the other slots are empty. Every row has a block of 512.
All inputs are finite; a program needn't handle non-finite values.
Results may differ from a plain program's by a relative error of at most 0.0003.
Values sent between devices are 32-bit elements; how exact they have to be, the bound alone decides.
No kernel may reach another device: no remote copies, remote signals or barrier semaphores. Data moves between devices by JAX's collectives and lax.ppermute only.
A program may use at most 64 MiB of HBM per device.

v0:
```python
import math
import jax
import jax.numpy as jnp
from jax import lax
from jax.sharding import PartitionSpec as P

ITERS = 2
rho_weight = 0.5
dual_rate = 0.1
balance_rate = 1.0


def apply_inverse(kkt_inverse, archetype, rhs_field, block_width):
    steps_count, rows_count = rhs_field.shape
    block_count = rows_count // block_width
    blocks_in = rhs_field.reshape(steps_count, block_count, block_width).transpose(1, 0, 2)
    labels_in = archetype.reshape(block_count, block_width)

    def one_block(operand):
        labels, columns_in = operand
        picked = jnp.take(kkt_inverse, labels, axis=0)
        return jnp.einsum("bts,sb->tb", picked, columns_in, precision=lax.Precision.HIGHEST)

    out_blocks = lax.map(one_block, (labels_in, blocks_in))
    return out_blocks.transpose(1, 0, 2).reshape(steps_count, rows_count)


def on_device(
    load_base, kkt_inverse, archetype, feeder, live_counts, feeder_cap, dual_start, balance_target
):
    steps_count, rows_count = load_base.shape
    block_total = lax.axis_size("dw")
    slot_width = rows_count // block_total
    owned_count = dual_start.shape[0]
    slot_index = jnp.arange(slot_width, dtype=jnp.int32)
    live_mask = (
        (live_counts.reshape(block_total, 1) > slot_index[None, :])
        .reshape(rows_count)
        .astype(jnp.float32)
    )
    all_rows = rows_count * block_total * lax.axis_size("reg")
    inv_root = 1.0 / math.sqrt(all_rows)
    block_width = math.gcd(rows_count, 256)
    local_label = feeder % owned_count
    cap_value = feeder_cap.astype(jnp.float32) * 0.001
    feeder_duals = dual_start
    balance_dual = jnp.zeros((steps_count,), jnp.float32)
    roster = jnp.zeros_like(load_base)
    contract_rows = (((0,), (1,)), ((), ()))
    arrived_labels = lax.all_to_all(local_label, "dw", split_axis=0, concat_axis=0, tiled=True)
    owner_table = (
        arrived_labels[:, None] == jnp.arange(owned_count, dtype=jnp.int32)[None, :]
    ).astype(jnp.float32)
    for sweep_index in range(ITERS):
        owner_rows = lax.dot_general(
            feeder_duals, owner_table, contract_rows, precision=lax.Precision.HIGHEST
        )
        dwelling_duals = lax.all_to_all(owner_rows, "dw", split_axis=1, concat_axis=1, tiled=True)
        rhs_field = load_base - dwelling_duals - balance_dual[:, None] + rho_weight * roster
        roster = apply_inverse(kkt_inverse, archetype, rhs_field, block_width) * live_mask[None, :]
        arrived_loads = lax.all_to_all(roster, "dw", split_axis=1, concat_axis=1, tiled=True)
        feeder_loads = lax.dot_general(
            owner_table, arrived_loads, contract_rows, precision=lax.Precision.HIGHEST
        )
        system_load = lax.psum(jnp.sum(feeder_loads, axis=0), ("dw", "reg"))
        feeder_duals = jnp.maximum(
            feeder_duals + dual_rate * (feeder_loads - cap_value[:, None]), 0.0
        )
        balance_dual = balance_dual + balance_rate * (system_load * inv_root - balance_target)
    return (roster, feeder_duals, balance_dual)


def solution(mesh):
    in_specs = (
        P(None, ("scen", "dw", "reg")),
        P(),
        P(("scen", "dw", "reg")),
        P(("scen", "dw", "reg")),
        P(("scen", "dw", "reg"), None),
        P(("scen", "dw", "reg")),
        P(("scen", "dw", "reg"), None),
        P("scen"),
    )
    out_specs = (P(None, ("scen", "dw", "reg")), P(("scen", "dw", "reg"), None), P("scen"))
    return jax.shard_map(
        on_device, mesh=mesh, in_specs=in_specs, out_specs=out_specs, check_vma=False
    )
```

profile of v0, /device:TPU:0, one launch (start us, length us, event | category | flops | bytes accessed | tf_op | source)
XLA Modules:
  0.0 417.4 jit_solution(971037340868108701)
XLA Ops:
  1.3 7.8 %all_to_all.51 = s32[4,512,1]{1,2,0:T(1,128)S(1)} all-to-all(s32[4,512,1]{1,2,0:T(1,128)S(1)} %bitcast.121), channel_id=1, replica_groups=mesh['scen'=2,'dw'=4,'reg'=4] {'dw'}, dimensions={0} | all-to-all | bytes 16384 | tf_op jit(solution)/shard_map/all_to_all | solution.py:50
  16.9 10.2 %all-to-all-done.1 = f32[96,4,512]{2,0,1:T(8,128)S(1)} async-done(((f32[96,4,512]{2,0,1:T(8,128)}), f32[96,4,512]{2,0,1:T(8,128)S(1)}, u32[]{:S(2)}, u32[]{:S(2)}) %all-to-all-start.1) | async-done | bytes 786464 | tf_op jit(solution)/shard_map/all_to_all | solution.py:58
  29.6 136.5 %while.20 = (s32[]{:T(128)}, f32[8,96,256]{2,1,0:T(8,128)}, f32[8,96,256]{2,0,1:T(8,128)S(1)}, s32[8,256]{1,0:T(8,128)S(1)}, f32[64,96,96]{2,1,0:T(8,128)}, /*index=5*/s32[]{:T(128)}) while((s32[]{:T(128)}, f32[8,96,256]{2,1,0:T(8,128)}, f32[8,96,256]{2,0,1:T(8,128)S(1)}, s32[8,256]{1,0:T(8,128)S(1)}, f32[64,96,96]{2,1,0:T(8,128)}, ...), condition=%wide.region_1.3_spmd, body=%wide.region_0.2_spmd.sunk | while | flops 7056642 | bytes 29306956 | solution.py:24
  29.6 7.8 %gather_fusion = f32[256,96,96]{2,1,0:T(8,128)} fusion(f32[64,96,96]{2,1,0:T(8,128)} %get-tuple-element.179, s32[1024]{0:T(1024)S(1)} %pad_clamp_fusion.4), kind=kCustom, calls=%fused_computation.clone.clone.1 | custom fusion | bytes 18875392 | tf_op jit(solution)/shard_map/while/body/eval_jaxpr/jit(_take)/gather | solution.py:21
  37.6 8.3 %multiply_reduce_fusion.4 = f32[256,96]{1,0:T(8,128)S(1)} fusion(f32[256,96,96]{2,1,0:T(8,128)} %gather_fusion, f32[256,96]{1,0:T(8,128)S(1)} %bitcast.87, pred[256]{0:T(512)(128)(4,1)S(1)} %compare_and_fusion.4), kind=kLoop, calls=%fused_computation.2.clone.1 | loop fusion | flops 7053312 | bytes 9634048 | tf_op jit(solution)/shard_map/while
  46.7 7.8 %gather_fusion = f32[256,96,96]{2,1,0:T(8,128)} fusion(f32[64,96,96]{2,1,0:T(8,128)} %get-tuple-element.179, s32[1024]{0:T(1024)S(1)} %pad_clamp_fusion.4), kind=kCustom, calls=%fused_computation.clone.clone.1 | custom fusion | bytes 18875392 | tf_op jit(solution)/shard_map/while/body/eval_jaxpr/jit(_take)/gather | solution.py:21
  54.7 8.3 %multiply_reduce_fusion.4 = f32[256,96]{1,0:T(8,128)S(1)} fusion(f32[256,96,96]{2,1,0:T(8,128)} %gather_fusion, f32[256,96]{1,0:T(8,128)S(1)} %bitcast.87, pred[256]{0:T(512)(128)(4,1)S(1)} %compare_and_fusion.4), kind=kLoop, calls=%fused_computation.2.clone.1 | loop fusion | flops 7053312 | bytes 9634048 | tf_op jit(solution)/shard_map/while
  63.7 7.8 %gather_fusion = f32[256,96,96]{2,1,0:T(8,128)} fusion(f32[64,96,96]{2,1,0:T(8,128)} %get-tuple-element.179, s32[1024]{0:T(1024)S(1)} %pad_clamp_fusion.4), kind=kCustom, calls=%fused_computation.clone.clone.1 | custom fusion | bytes 18875392 | tf_op jit(solution)/shard_map/while/body/eval_jaxpr/jit(_take)/gather | solution.py:21
  71.7 8.3 %multiply_reduce_fusion.4 = f32[256,96]{1,0:T(8,128)S(1)} fusion(f32[256,96,96]{2,1,0:T(8,128)} %gather_fusion, f32[256,96]{1,0:T(8,128)S(1)} %bitcast.87, pred[256]{0:T(512)(128)(4,1)S(1)} %compare_and_fusion.4), kind=kLoop, calls=%fused_computation.2.clone.1 | loop fusion | flops 7053312 | bytes 9634048 | tf_op jit(solution)/shard_map/while
  80.8 7.8 %gather_fusion = f32[256,96,96]{2,1,0:T(8,128)} fusion(f32[64,96,96]{2,1,0:T(8,128)} %get-tuple-element.179, s32[1024]{0:T(1024)S(1)} %pad_clamp_fusion.4), kind=kCustom, calls=%fused_computation.clone.clone.1 | custom fusion | bytes 18875392 | tf_op jit(solution)/shard_map/while/body/eval_jaxpr/jit(_take)/gather | solution.py:21
  88.8 8.3 %multiply_reduce_fusion.4 = f32[256,96]{1,0:T(8,128)S(1)} fusion(f32[256,96,96]{2,1,0:T(8,128)} %gather_fusion, f32[256,96]{1,0:T(8,128)S(1)} %bitcast.87, pred[256]{0:T(512)(128)(4,1)S(1)} %compare_and_fusion.4), kind=kLoop, calls=%fused_computation.2.clone.1 | loop fusion | flops 7053312 | bytes 9634048 | tf_op jit(solution)/shard_map/while
  97.8 7.8 %gather_fusion = f32[256,96,96]{2,1,0:T(8,128)} fusion(f32[64,96,96]{2,1,0:T(8,128)} %get-tuple-element.179, s32[1024]{0:T(1024)S(1)} %pad_clamp_fusion.4), kind=kCustom, calls=%fused_computation.clone.clone.1 | custom fusion | bytes 18875392 | tf_op jit(solution)/shard_map/while/body/eval_jaxpr/jit(_take)/gather | solution.py:21
  105.8 8.3 %multiply_reduce_fusion.4 = f32[256,96]{1,0:T(8,128)S(1)} fusion(f32[256,96,96]{2,1,0:T(8,128)} %gather_fusion, f32[256,96]{1,0:T(8,128)S(1)} %bitcast.87, pred[256]{0:T(512)(128)(4,1)S(1)} %compare_and_fusion.4), kind=kLoop, calls=%fused_computation.2.clone.1 | loop fusion | flops 7053312 | bytes 9634048 | tf_op jit(solution)/shard_map/while
  114.9 7.8 %gather_fusion = f32[256,96,96]{2,1,0:T(8,128)} fusion(f32[64,96,96]{2,1,0:T(8,128)} %get-tuple-element.179, s32[1024]{0:T(1024)S(1)} %pad_clamp_fusion.4), kind=kCustom, calls=%fused_computation.clone.clone.1 | custom fusion | bytes 18875392 | tf_op jit(solution)/shard_map/while/body/eval_jaxpr/jit(_take)/gather | solution.py:21
  122.9 8.3 %multiply_reduce_fusion.4 = f32[256,96]{1,0:T(8,128)S(1)} fusion(f32[256,96,96]{2,1,0:T(8,128)} %gather_fusion, f32[256,96]{1,0:T(8,128)S(1)} %bitcast.87, pred[256]{0:T(512)(128)(4,1)S(1)} %compare_and_fusion.4), kind=kLoop, calls=%fused_computation.2.clone.1 | loop fusion | flops 7053312 | bytes 9634048 | tf_op jit(solution)/shard_map/while
  131.9 7.8 %gather_fusion = f32[256,96,96]{2,1,0:T(8,128)} fusion(f32[64,96,96]{2,1,0:T(8,128)} %get-tuple-element.179, s32[1024]{0:T(1024)S(1)} %pad_clamp_fusion.4), kind=kCustom, calls=%fused_computation.clone.clone.1 | custom fusion | bytes 18875392 | tf_op jit(solution)/shard_map/while/body/eval_jaxpr/jit(_take)/gather | solution.py:21
  140.0 8.3 %multiply_reduce_fusion.4 = f32[256,96]{1,0:T(8,128)S(1)} fusion(f32[256,96,96]{2,1,0:T(8,128)} %gather_fusion, f32[256,96]{1,0:T(8,128)S(1)} %bitcast.87, pred[256]{0:T(512)(128)(4,1)S(1)} %compare_and_fusion.4), kind=kLoop, calls=%fused_computation.2.clone.1 | loop fusion | flops 7053312 | bytes 9634048 | tf_op jit(solution)/shard_map/while
  149.0 7.8 %gather_fusion = f32[256,96,96]{2,1,0:T(8,128)} fusion(f32[64,96,96]{2,1,0:T(8,128)} %get-tuple-element.179, s32[1024]{0:T(1024)S(1)} %pad_clamp_fusion.4), kind=kCustom, calls=%fused_computation.clone.clone.1 | custom fusion | bytes 18875392 | tf_op jit(solution)/shard_map/while/body/eval_jaxpr/jit(_take)/gather | solution.py:21
  157.0 8.3 %multiply_reduce_fusion.4 = f32[256,96]{1,0:T(8,128)S(1)} fusion(f32[256,96,96]{2,1,0:T(8,128)} %gather_fusion, f32[256,96]{1,0:T(8,128)S(1)} %bitcast.87, pred[256]{0:T(512)(128)(4,1)S(1)} %compare_and_fusion.4), kind=kLoop, calls=%fused_computation.2.clone.1 | loop fusion | flops 7053312 | bytes 9634048 | tf_op jit(solution)/shard_map/while
  177.6 11.7 %all-to-all-done.2 = f32[96,4,512]{2,0,1:T(8,128)} async-done(((f32[96,4,512]{2,0,1:T(8,128)}), f32[96,4,512]{2,0,1:T(8,128)}, u32[]{:S(2)}, u32[]{:S(2)}) %all-to-all-start.2) | async-done | bytes 786464 | tf_op jit(solution)/shard_map/all_to_all | solution.py:61
  199.9 34.7 %psum.14 = f32[96]{0:T(128)S(1)} all-reduce(f32[96]{0:T(128)S(1)} %get-tuple-element.99), channel_id=1, replica_groups=mesh['scen'=2,'dw'=4,'reg'=4] {'dw','reg'}, use_global_device_ids=true, to_apply=%region_3.5 | all-reduce | flops 96 | bytes 768 | tf_op jit(solution)/shard_map/psum | solution.py:65
  239.3 127.9 %while.21 = (s32[]{:T(128)}, f32[8,96,256]{2,1,0:T(8,128)}, f32[8,96,256]{2,1,0:T(8,128)}, s32[8,256]{1,0:T(8,128)S(1)}, f32[64,96,96]{2,1,0:T(8,128)S(1)}, /*index=5*/s32[]{:T(128)}) while((s32[]{:T(128)}, f32[8,96,256]{2,1,0:T(8,128)}, f32[8,96,256]{2,1,0:T(8,128)}, s32[8,256]{1,0:T(8,128)S(1)}, f32[64,96,96]{2,1,0:T(8,128)S(1)}, ...), condition=%wide.region_5.7_spmd, body=%wide.region_4.6_spmd.sunk | while | flops 7056642 | bytes 29306956 | solution.py:24
  246.3 8.3 %multiply_reduce_fusion.5 = f32[256,96]{1,0:T(8,128)S(1)} fusion(f32[256,96,96]{2,1,0:T(8,128)} %gather_fusion.1, f32[256,96]{1,0:T(8,128)S(1)} %copy.85, pred[256]{0:T(512)(128)(4,1)S(1)} %compare_and_fusion.5), kind=kLoop, calls=%fused_computation.9.clone.1 | loop fusion | flops 7053312 | bytes 9634048 | tf_op jit(solution)/shard_map/while
  262.3 8.3 %multiply_reduce_fusion.5 = f32[256,96]{1,0:T(8,128)S(1)} fusion(f32[256,96,96]{2,1,0:T(8,128)} %gather_fusion.1, f32[256,96]{1,0:T(8,128)S(1)} %copy.85, pred[256]{0:T(512)(128)(4,1)S(1)} %compare_and_fusion.5), kind=kLoop, calls=%fused_computation.9.clone.1 | loop fusion | flops 7053312 | bytes 9634048 | tf_op jit(solution)/shard_map/while
  278.3 8.3 %multiply_reduce_fusion.5 = f32[256,96]{1,0:T(8,128)S(1)} fusion(f32[256,96,96]{2,1,0:T(8,128)} %gather_fusion.1, f32[256,96]{1,0:T(8,128)S(1)} %copy.85, pred[256]{0:T(512)(128)(4,1)S(1)} %compare_and_fusion.5), kind=kLoop, calls=%fused_computation.9.clone.1 | loop fusion | flops 7053312 | bytes 9634048 | tf_op jit(solution)/shard_map/while
  294.2 8.3 %multiply_reduce_fusion.5 = f32[256,96]{1,0:T(8,128)S(1)} fusion(f32[256,96,96]{2,1,0:T(8,128)} %gather_fusion.1, f32[256,96]{1,0:T(8,128)S(1)} %copy.85, pred[256]{0:T(512)(128)(4,1)S(1)} %compare_and_fusion.5), kind=kLoop, calls=%fused_computation.9.clone.1 | loop fusion | flops 7053312 | bytes 9634048 | tf_op jit(solution)/shard_map/while
  310.2 8.3 %multiply_reduce_fusion.5 = f32[256,96]{1,0:T(8,128)S(1)} fusion(f32[256,96,96]{2,1,0:T(8,128)} %gather_fusion.1, f32[256,96]{1,0:T(8,128)S(1)} %copy.85, pred[256]{0:T(512)(128)(4,1)S(1)} %compare_and_fusion.5), kind=kLoop, calls=%fused_computation.9.clone.1 | loop fusion | flops 7053312 | bytes 9634048 | tf_op jit(solution)/shard_map/while
  326.2 8.3 %multiply_reduce_fusion.5 = f32[256,96]{1,0:T(8,128)S(1)} fusion(f32[256,96,96]{2,1,0:T(8,128)} %gather_fusion.1, f32[256,96]{1,0:T(8,128)S(1)} %copy.85, pred[256]{0:T(512)(128)(4,1)S(1)} %compare_and_fusion.5), kind=kLoop, calls=%fused_computation.9.clone.1 | loop fusion | flops 7053312 | bytes 9634048 | tf_op jit(solution)/shard_map/while
  342.2 8.3 %multiply_reduce_fusion.5 = f32[256,96]{1,0:T(8,128)S(1)} fusion(f32[256,96,96]{2,1,0:T(8,128)} %gather_fusion.1, f32[256,96]{1,0:T(8,128)S(1)} %copy.85, pred[256]{0:T(512)(128)(4,1)S(1)} %compare_and_fusion.5), kind=kLoop, calls=%fused_computation.9.clone.1 | loop fusion | flops 7053312 | bytes 9634048 | tf_op jit(solution)/shard_map/while
  358.2 8.3 %multiply_reduce_fusion.5 = f32[256,96]{1,0:T(8,128)S(1)} fusion(f32[256,96,96]{2,1,0:T(8,128)} %gather_fusion.1, f32[256,96]{1,0:T(8,128)S(1)} %copy.85, pred[256]{0:T(512)(128)(4,1)S(1)} %compare_and_fusion.5), kind=kLoop, calls=%fused_computation.9.clone.1 | loop fusion | flops 7053312 | bytes 9634048 | tf_op jit(solution)/shard_map/while
  376.1 9.5 %all-to-all-done.4 = f32[96,4,512]{2,0,1:T(8,128)S(1)} async-done(((f32[96,4,512]{2,0,1:T(8,128)}), f32[96,4,512]{2,0,1:T(8,128)S(1)}, u32[]{:S(2)}, u32[]{:S(2)}) %all-to-all-start.4) | async-done | bytes 786464 | tf_op jit(solution)/shard_map/all_to_all | solution.py:61
  387.3 29.7 %psum.15 = f32[96]{0:T(128)S(1)} all-reduce(f32[96]{0:T(128)S(1)} %get-tuple-element.95), channel_id=1, replica_groups=mesh['scen'=2,'dw'=4,'reg'=4] {'dw','reg'}, use_global_device_ids=true, to_apply=%region_7.9 | all-reduce | flops 96 | bytes 768 | tf_op jit(solution)/shard_map/psum | solution.py:65
  (185 shorter events, 117.7 us)
Async XLA Ops:
  11.9 15.1 %all-to-all-start.1 = ((f32[96,4,512]{2,0,1:T(8,128)}), f32[96,4,512]{2,0,1:T(8,128)S(1)}, u32[]{:S(2)}, u32[]{:S(2)}) async-start(f32[96,4,512]{2,0,1:T(8,128)} %bitcast.64), calls=%async_computation.1 | async-start | bytes 1572864 | tf_op jit(solution)/shard_map/all_to_all | solution.py:58
  29.6 148.1 %copy-start.3 = (s32[16]{0:T(128)S(1)}, s32[16]{0:T(128)}, u32[]{:S(2)}) copy-start(s32[16]{0:T(128)} %param.19) | copy-start | bytes 196
  29.6 162.0 %copy-start.1 = (f32[16,96]{1,0:T(8,128)S(1)}, f32[16,96]{1,0:T(8,128)}, u32[]{:S(2)}) copy-start(f32[16,96]{1,0:T(8,128)} %param.20) | copy-start | bytes 18436
  166.0 68.5 %copy-start.2 = (f32[96]{0:T(128)S(1)}, f32[96]{0:T(128)}, u32[]{:S(2)}) copy-start(f32[96]{0:T(128)} %param.21) | copy-start | bytes 1156
  166.0 73.3 %copy-start = (f32[64,96,96]{2,1,0:T(8,128)S(1)}, f32[64,96,96]{2,1,0:T(8,128)}, u32[]{:S(2)}) copy-start(f32[64,96,96]{2,1,0:T(8,128)} %get-tuple-element.199) | copy-start | bytes 7077892
  173.4 15.9 %all-to-all-start.2 = ((f32[96,4,512]{2,0,1:T(8,128)}), f32[96,4,512]{2,0,1:T(8,128)}, u32[]{:S(2)}, u32[]{:S(2)}) async-start(f32[96,4,512]{2,0,1:T(8,128)} %copy.36), calls=%async_computation.2 | async-start | bytes 1572864 | tf_op jit(solution)/shard_map/all_to_all | solution.py:61
  193.5 41.0 %all-to-all-start.3 = ((f32[96,4,512]{2,0,1:T(8,128)}), f32[96,4,512]{2,0,1:T(8,128)}, u32[]{:S(2)}, u32[]{:S(2)}) async-start(f32[96,4,512]{2,0,1:T(8,128)} %bitcast.91), calls=%async_computation.3 | async-start | bytes 1572864 | tf_op jit(solution)/shard_map/all_to_all | solution.py:58
  370.4 15.1 %all-to-all-start.4 = ((f32[96,4,512]{2,0,1:T(8,128)}), f32[96,4,512]{2,0,1:T(8,128)S(1)}, u32[]{:S(2)}, u32[]{:S(2)}) async-start(f32[96,4,512]{2,0,1:T(8,128)} %copy.44), calls=%async_computation.4 | async-start | bytes 1572864 | tf_op jit(solution)/shard_map/all_to_all | solution.py:61
where the time goes:
time: 419 us; the launch traced here: 417 us
  local copies, waits for them, and re-layouts  152 us (36%)
  other arithmetic  140 us (33%)
  blocking collectives  72.1 us (17%)
  waiting for transfers between devices  31.3 us (7%)
  starting transfers between devices  15.4 us (4%)
  matrix products  5.55 us (1%)
    while x16, other arithmetic  132 us
    gather x16, local copies, waits for them, and re-layouts, one_block(): picked = jnp.take(kkt_inverse, labels, axis=0)  110 us
    psum x2, blocking collectives, on_device(): system_load = lax.psum(jnp.sum(feeder_loads, axis=0), ('dw', 'reg'))  64.3 us
    all_to_all x2, waiting for transfers between devices, on_device(): lax.all_to_all(roster, 'dw', split_axis=1, concat_axis=1, tiled=True)  21.1 us
    dynamic_update_slice x16, local copies, waits for them, and re-layouts, apply_inverse(): out_blocks = lax.map(one_block, (labels_in, blocks_in))  10.5 us
    all_to_all x2, waiting for transfers between devices, on_device(): lax.all_to_all(owner_rows, 'dw', split_axis=1, concat_axis=1, tiled=True)  10.2 us
    while x24, local copies, waits for them, and re-layouts  8.65 us
  transfers between devices with their start and end apart: 4, of which 3 were waited for; matrix products, arithmetic and copies ran while one was open for 1% of the time, Pallas kernels for 0%

commit v1 on v0

--- a/solution.py
+++ b/solution.py
@@ -62,7 +62,8 @@
         feeder_loads = lax.dot_general(
             owner_table, arrived_loads, contract_rows, precision=lax.Precision.HIGHEST
         )
-        system_load = lax.psum(jnp.sum(feeder_loads, axis=0), ("dw", "reg"))
+        half = lax.psum(jnp.sum(feeder_loads, axis=0), "reg")
+        system_load = lax.psum(half, "dw")
         feeder_duals = jnp.maximum(
             feeder_duals + dual_rate * (feeder_loads - cap_value[:, None]), 0.0
         )

time: 419 us -> 387 us (0.924)
  blocking collectives: 72.1 us -> 39.6 us
    psum x2 -> x4, blocking collectives: 64.3 us -> 31.8 us  [the longest x2 20.3 us: on_device(): half = lax.psum(jnp.sum(feeder_loads, axis=0), 'reg')]
where the time goes in v1:
time: 387 us; the launch traced here: 385 us
  local copies, waits for them, and re-layouts  152 us (39%)
  other arithmetic  140 us (36%)
  blocking collectives  39.6 us (10%)
  waiting for transfers between devices  31.3 us (8%)
  starting transfers between devices  15.4 us (4%)
  matrix products  5.55 us (1%)
    while x16, other arithmetic  132 us
    gather x16, local copies, waits for them, and re-layouts, one_block(): picked = jnp.take(kkt_inverse, labels, axis=0)  110 us
    all_to_all x2, waiting for transfers between devices, on_device(): lax.all_to_all(roster, 'dw', split_axis=1, concat_axis=1, tiled=True)  21.1 us
    psum x2, blocking collectives, on_device(): half = lax.psum(jnp.sum(feeder_loads, axis=0), 'reg')  20.3 us
    psum x2, blocking collectives, on_device(): system_load = lax.psum(half, 'dw')  11.6 us
    dynamic_update_slice x16, local copies, waits for them, and re-layouts, apply_inverse(): out_blocks = lax.map(one_block, (labels_in, blocks_in))  10.5 us
    all_to_all x2, waiting for transfers between devices, on_device(): lax.all_to_all(owner_rows, 'dw', split_axis=1, concat_axis=1, tiled=True)  10.2 us
    while x24, local copies, waits for them, and re-layouts  8.65 us
  transfers between devices with their start and end apart: 4, of which 3 were waited for; matrix products, arithmetic and copies ran while one was open for 1% of the time, Pallas kernels for 0%

profile of v1, /device:TPU:0, one launch (start us, length us, event | category | flops | bytes accessed | tf_op | source)
XLA Modules:
  0.0 385.0 jit_solution(650307552702069709)
XLA Ops:
  1.3 7.8 %all_to_all.51 = s32[4,512,1]{1,2,0:T(1,128)S(1)} all-to-all(s32[4,512,1]{1,2,0:T(1,128)S(1)} %bitcast.121), channel_id=1, replica_groups=mesh['scen'=2,'dw'=4,'reg'=4] {'dw'}, dimensions={0} | all-to-all | bytes 16384 | tf_op jit(solution)/shard_map/all_to_all | solution.py:50
  16.9 10.2 %all-to-all-done.1 = f32[96,4,512]{2,0,1:T(8,128)S(1)} async-done(((f32[96,4,512]{2,0,1:T(8,128)}), f32[96,4,512]{2,0,1:T(8,128)S(1)}, u32[]{:S(2)}, u32[]{:S(2)}) %all-to-all-start.1) | async-done | bytes 786464 | tf_op jit(solution)/shard_map/all_to_all | solution.py:58
  29.6 136.5 %while.20 = (s32[]{:T(128)}, f32[8,96,256]{2,1,0:T(8,128)}, f32[8,96,256]{2,0,1:T(8,128)S(1)}, s32[8,256]{1,0:T(8,128)S(1)}, f32[64,96,96]{2,1,0:T(8,128)}, /*index=5*/s32[]{:T(128)}) while((s32[]{:T(128)}, f32[8,96,256]{2,1,0:T(8,128)}, f32[8,96,256]{2,0,1:T(8,128)S(1)}, s32[8,256]{1,0:T(8,128)S(1)}, f32[64,96,96]{2,1,0:T(8,128)}, ...), condition=%wide.region_1.3_spmd, body=%wide.region_0.2_spmd.sunk | while | flops 7056642 | bytes 29306956 | solution.py:24
  29.6 7.8 %gather_fusion = f32[256,96,96]{2,1,0:T(8,128)} fusion(f32[64,96,96]{2,1,0:T(8,128)} %get-tuple-element.179, s32[1024]{0:T(1024)S(1)} %pad_clamp_fusion.4), kind=kCustom, calls=%fused_computation.clone.clone.1 | custom fusion | bytes 18875392 | tf_op jit(solution)/shard_map/while/body/eval_jaxpr/jit(_take)/gather | solution.py:21
  37.6 8.3 %multiply_reduce_fusion.4 = f32[256,96]{1,0:T(8,128)S(1)} fusion(f32[256,96,96]{2,1,0:T(8,128)} %gather_fusion, f32[256,96]{1,0:T(8,128)S(1)} %bitcast.87, pred[256]{0:T(512)(128)(4,1)S(1)} %compare_and_fusion.4), kind=kLoop, calls=%fused_computation.2.clone.1 | loop fusion | flops 7053312 | bytes 9634048 | tf_op jit(solution)/shard_map/while
  46.7 7.8 %gather_fusion = f32[256,96,96]{2,1,0:T(8,128)} fusion(f32[64,96,96]{2,1,0:T(8,128)} %get-tuple-element.179, s32[1024]{0:T(1024)S(1)} %pad_clamp_fusion.4), kind=kCustom, calls=%fused_computation.clone.clone.1 | custom fusion | bytes 18875392 | tf_op jit(solution)/shard_map/while/body/eval_jaxpr/jit(_take)/gather | solution.py:21
  54.7 8.3 %multiply_reduce_fusion.4 = f32[256,96]{1,0:T(8,128)S(1)} fusion(f32[256,96,96]{2,1,0:T(8,128)} %gather_fusion, f32[256,96]{1,0:T(8,128)S(1)} %bitcast.87, pred[256]{0:T(512)(128)(4,1)S(1)} %compare_and_fusion.4), kind=kLoop, calls=%fused_computation.2.clone.1 | loop fusion | flops 7053312 | bytes 9634048 | tf_op jit(solution)/shard_map/while
  63.7 7.8 %gather_fusion = f32[256,96,96]{2,1,0:T(8,128)} fusion(f32[64,96,96]{2,1,0:T(8,128)} %get-tuple-element.179, s32[1024]{0:T(1024)S(1)} %pad_clamp_fusion.4), kind=kCustom, calls=%fused_computation.clone.clone.1 | custom fusion | bytes 18875392 | tf_op jit(solution)/shard_map/while/body/eval_jaxpr/jit(_take)/gather | solution.py:21
  71.7 8.3 %multiply_reduce_fusion.4 = f32[256,96]{1,0:T(8,128)S(1)} fusion(f32[256,96,96]{2,1,0:T(8,128)} %gather_fusion, f32[256,96]{1,0:T(8,128)S(1)} %bitcast.87, pred[256]{0:T(512)(128)(4,1)S(1)} %compare_and_fusion.4), kind=kLoop, calls=%fused_computation.2.clone.1 | loop fusion | flops 7053312 | bytes 9634048 | tf_op jit(solution)/shard_map/while
  80.8 7.8 %gather_fusion = f32[256,96,96]{2,1,0:T(8,128)} fusion(f32[64,96,96]{2,1,0:T(8,128)} %get-tuple-element.179, s32[1024]{0:T(1024)S(1)} %pad_clamp_fusion.4), kind=kCustom, calls=%fused_computation.clone.clone.1 | custom fusion | bytes 18875392 | tf_op jit(solution)/shard_map/while/body/eval_jaxpr/jit(_take)/gather | solution.py:21
  88.8 8.3 %multiply_reduce_fusion.4 = f32[256,96]{1,0:T(8,128)S(1)} fusion(f32[256,96,96]{2,1,0:T(8,128)} %gather_fusion, f32[256,96]{1,0:T(8,128)S(1)} %bitcast.87, pred[256]{0:T(512)(128)(4,1)S(1)} %compare_and_fusion.4), kind=kLoop, calls=%fused_computation.2.clone.1 | loop fusion | flops 7053312 | bytes 9634048 | tf_op jit(solution)/shard_map/while
  97.8 7.8 %gather_fusion = f32[256,96,96]{2,1,0:T(8,128)} fusion(f32[64,96,96]{2,1,0:T(8,128)} %get-tuple-element.179, s32[1024]{0:T(1024)S(1)} %pad_clamp_fusion.4), kind=kCustom, calls=%fused_computation.clone.clone.1 | custom fusion | bytes 18875392 | tf_op jit(solution)/shard_map/while/body/eval_jaxpr/jit(_take)/gather | solution.py:21
  105.8 8.3 %multiply_reduce_fusion.4 = f32[256,96]{1,0:T(8,128)S(1)} fusion(f32[256,96,96]{2,1,0:T(8,128)} %gather_fusion, f32[256,96]{1,0:T(8,128)S(1)} %bitcast.87, pred[256]{0:T(512)(128)(4,1)S(1)} %compare_and_fusion.4), kind=kLoop, calls=%fused_computation.2.clone.1 | loop fusion | flops 7053312 | bytes 9634048 | tf_op jit(solution)/shard_map/while
  114.9 7.8 %gather_fusion = f32[256,96,96]{2,1,0:T(8,128)} fusion(f32[64,96,96]{2,1,0:T(8,128)} %get-tuple-element.179, s32[1024]{0:T(1024)S(1)} %pad_clamp_fusion.4), kind=kCustom, calls=%fused_computation.clone.clone.1 | custom fusion | bytes 18875392 | tf_op jit(solution)/shard_map/while/body/eval_jaxpr/jit(_take)/gather | solution.py:21
  122.9 8.3 %multiply_reduce_fusion.4 = f32[256,96]{1,0:T(8,128)S(1)} fusion(f32[256,96,96]{2,1,0:T(8,128)} %gather_fusion, f32[256,96]{1,0:T(8,128)S(1)} %bitcast.87, pred[256]{0:T(512)(128)(4,1)S(1)} %compare_and_fusion.4), kind=kLoop, calls=%fused_computation.2.clone.1 | loop fusion | flops 7053312 | bytes 9634048 | tf_op jit(solution)/shard_map/while
  131.9 7.8 %gather_fusion = f32[256,96,96]{2,1,0:T(8,128)} fusion(f32[64,96,96]{2,1,0:T(8,128)} %get-tuple-element.179, s32[1024]{0:T(1024)S(1)} %pad_clamp_fusion.4), kind=kCustom, calls=%fused_computation.clone.clone.1 | custom fusion | bytes 18875392 | tf_op jit(solution)/shard_map/while/body/eval_jaxpr/jit(_take)/gather | solution.py:21
  140.0 8.3 %multiply_reduce_fusion.4 = f32[256,96]{1,0:T(8,128)S(1)} fusion(f32[256,96,96]{2,1,0:T(8,128)} %gather_fusion, f32[256,96]{1,0:T(8,128)S(1)} %bitcast.87, pred[256]{0:T(512)(128)(4,1)S(1)} %compare_and_fusion.4), kind=kLoop, calls=%fused_computation.2.clone.1 | loop fusion | flops 7053312 | bytes 9634048 | tf_op jit(solution)/shard_map/while
  149.0 7.8 %gather_fusion = f32[256,96,96]{2,1,0:T(8,128)} fusion(f32[64,96,96]{2,1,0:T(8,128)} %get-tuple-element.179, s32[1024]{0:T(1024)S(1)} %pad_clamp_fusion.4), kind=kCustom, calls=%fused_computation.clone.clone.1 | custom fusion | bytes 18875392 | tf_op jit(solution)/shard_map/while/body/eval_jaxpr/jit(_take)/gather | solution.py:21
  157.0 8.3 %multiply_reduce_fusion.4 = f32[256,96]{1,0:T(8,128)S(1)} fusion(f32[256,96,96]{2,1,0:T(8,128)} %gather_fusion, f32[256,96]{1,0:T(8,128)S(1)} %bitcast.87, pred[256]{0:T(512)(128)(4,1)S(1)} %compare_and_fusion.4), kind=kLoop, calls=%fused_computation.2.clone.1 | loop fusion | flops 7053312 | bytes 9634048 | tf_op jit(solution)/shard_map/while
  177.6 11.7 %all-to-all-done.2 = f32[96,4,512]{2,0,1:T(8,128)} async-done(((f32[96,4,512]{2,0,1:T(8,128)}), f32[96,4,512]{2,0,1:T(8,128)}, u32[]{:S(2)}, u32[]{:S(2)}) %all-to-all-start.2) | async-done | bytes 786464 | tf_op jit(solution)/shard_map/all_to_all | solution.py:61
  199.9 11.9 %psum.28 = f32[96]{0:T(128)S(1)} all-reduce(f32[96]{0:T(128)S(1)} %get-tuple-element.99), channel_id=1, replica_groups=mesh['scen'=2,'dw'=4,'reg'=4] {'reg'}, use_global_device_ids=true, to_apply=%region_3.5 | all-reduce | flops 96 | bytes 768 | tf_op jit(solution)/shard_map/psum | solution.py:65
  222.4 127.9 %while.21 = (s32[]{:T(128)}, f32[8,96,256]{2,1,0:T(8,128)}, f32[8,96,256]{2,1,0:T(8,128)}, s32[8,256]{1,0:T(8,128)S(1)}, f32[64,96,96]{2,1,0:T(8,128)S(1)}, /*index=5*/s32[]{:T(128)}) while((s32[]{:T(128)}, f32[8,96,256]{2,1,0:T(8,128)}, f32[8,96,256]{2,1,0:T(8,128)}, s32[8,256]{1,0:T(8,128)S(1)}, f32[64,96,96]{2,1,0:T(8,128)S(1)}, ...), condition=%wide.region_6.8_spmd, body=%wide.region_5.7_spmd.sunk | while | flops 7056642 | bytes 29306956 | solution.py:24
  229.4 8.3 %multiply_reduce_fusion.5 = f32[256,96]{1,0:T(8,128)S(1)} fusion(f32[256,96,96]{2,1,0:T(8,128)} %gather_fusion.1, f32[256,96]{1,0:T(8,128)S(1)} %copy.85, pred[256]{0:T(512)(128)(4,1)S(1)} %compare_and_fusion.5), kind=kLoop, calls=%fused_computation.9.clone.1 | loop fusion | flops 7053312 | bytes 9634048 | tf_op jit(solution)/shard_map/while
  245.4 8.3 %multiply_reduce_fusion.5 = f32[256,96]{1,0:T(8,128)S(1)} fusion(f32[256,96,96]{2,1,0:T(8,128)} %gather_fusion.1, f32[256,96]{1,0:T(8,128)S(1)} %copy.85, pred[256]{0:T(512)(128)(4,1)S(1)} %compare_and_fusion.5), kind=kLoop, calls=%fused_computation.9.clone.1 | loop fusion | flops 7053312 | bytes 9634048 | tf_op jit(solution)/shard_map/while
  261.4 8.3 %multiply_reduce_fusion.5 = f32[256,96]{1,0:T(8,128)S(1)} fusion(f32[256,96,96]{2,1,0:T(8,128)} %gather_fusion.1, f32[256,96]{1,0:T(8,128)S(1)} %copy.85, pred[256]{0:T(512)(128)(4,1)S(1)} %compare_and_fusion.5), kind=kLoop, calls=%fused_computation.9.clone.1 | loop fusion | flops 7053312 | bytes 9634048 | tf_op jit(solution)/shard_map/while
  277.3 8.3 %multiply_reduce_fusion.5 = f32[256,96]{1,0:T(8,128)S(1)} fusion(f32[256,96,96]{2,1,0:T(8,128)} %gather_fusion.1, f32[256,96]{1,0:T(8,128)S(1)} %copy.85, pred[256]{0:T(512)(128)(4,1)S(1)} %compare_and_fusion.5), kind=kLoop, calls=%fused_computation.9.clone.1 | loop fusion | flops 7053312 | bytes 9634048 | tf_op jit(solution)/shard_map/while
  293.3 8.3 %multiply_reduce_fusion.5 = f32[256,96]{1,0:T(8,128)S(1)} fusion(f32[256,96,96]{2,1,0:T(8,128)} %gather_fusion.1, f32[256,96]{1,0:T(8,128)S(1)} %copy.85, pred[256]{0:T(512)(128)(4,1)S(1)} %compare_and_fusion.5), kind=kLoop, calls=%fused_computation.9.clone.1 | loop fusion | flops 7053312 | bytes 9634048 | tf_op jit(solution)/shard_map/while
  309.3 8.3 %multiply_reduce_fusion.5 = f32[256,96]{1,0:T(8,128)S(1)} fusion(f32[256,96,96]{2,1,0:T(8,128)} %gather_fusion.1, f32[256,96]{1,0:T(8,128)S(1)} %copy.85, pred[256]{0:T(512)(128)(4,1)S(1)} %compare_and_fusion.5), kind=kLoop, calls=%fused_computation.9.clone.1 | loop fusion | flops 7053312 | bytes 9634048 | tf_op jit(solution)/shard_map/while
  325.3 8.3 %multiply_reduce_fusion.5 = f32[256,96]{1,0:T(8,128)S(1)} fusion(f32[256,96,96]{2,1,0:T(8,128)} %gather_fusion.1, f32[256,96]{1,0:T(8,128)S(1)} %copy.85, pred[256]{0:T(512)(128)(4,1)S(1)} %compare_and_fusion.5), kind=kLoop, calls=%fused_computation.9.clone.1 | loop fusion | flops 7053312 | bytes 9634048 | tf_op jit(solution)/shard_map/while
  341.3 8.3 %multiply_reduce_fusion.5 = f32[256,96]{1,0:T(8,128)S(1)} fusion(f32[256,96,96]{2,1,0:T(8,128)} %gather_fusion.1, f32[256,96]{1,0:T(8,128)S(1)} %copy.85, pred[256]{0:T(512)(128)(4,1)S(1)} %compare_and_fusion.5), kind=kLoop, calls=%fused_computation.9.clone.1 | loop fusion | flops 7053312 | bytes 9634048 | tf_op jit(solution)/shard_map/while
  359.2 9.5 %all-to-all-done.4 = f32[96,4,512]{2,0,1:T(8,128)S(1)} async-done(((f32[96,4,512]{2,0,1:T(8,128)}), f32[96,4,512]{2,0,1:T(8,128)S(1)}, u32[]{:S(2)}, u32[]{:S(2)}) %all-to-all-start.4) | async-done | bytes 786464 | tf_op jit(solution)/shard_map/all_to_all | solution.py:61
  370.4 8.3 %psum.30 = f32[96]{0:T(128)S(1)} all-reduce(f32[96]{0:T(128)S(1)} %get-tuple-element.95), channel_id=1, replica_groups=mesh['scen'=2,'dw'=4,'reg'=4] {'reg'}, use_global_device_ids=true, to_apply=%region_8.10 | all-reduce | flops 96 | bytes 768 | tf_op jit(solution)/shard_map/psum | solution.py:65
  (187 shorter events, 129.3 us)
Async XLA Ops:
  11.9 15.1 %all-to-all-start.1 = ((f32[96,4,512]{2,0,1:T(8,128)}), f32[96,4,512]{2,0,1:T(8,128)S(1)}, u32[]{:S(2)}, u32[]{:S(2)}) async-start(f32[96,4,512]{2,0,1:T(8,128)} %bitcast.64), calls=%async_computation.1 | async-start | bytes 1572864 | tf_op jit(solution)/shard_map/all_to_all | solution.py:58
  29.6 148.1 %copy-start.3 = (s32[16]{0:T(128)S(1)}, s32[16]{0:T(128)}, u32[]{:S(2)}) copy-start(s32[16]{0:T(128)} %param.19) | copy-start | bytes 196
  29.6 162.0 %copy-start.1 = (f32[16,96]{1,0:T(8,128)S(1)}, f32[16,96]{1,0:T(8,128)}, u32[]{:S(2)}) copy-start(f32[16,96]{1,0:T(8,128)} %param.20) | copy-start | bytes 18436
  166.0 51.6 %copy-start.2 = (f32[96]{0:T(128)S(1)}, f32[96]{0:T(128)}, u32[]{:S(2)}) copy-start(f32[96]{0:T(128)} %param.21) | copy-start | bytes 1156
  166.0 56.4 %copy-start = (f32[64,96,96]{2,1,0:T(8,128)S(1)}, f32[64,96,96]{2,1,0:T(8,128)}, u32[]{:S(2)}) copy-start(f32[64,96,96]{2,1,0:T(8,128)} %get-tuple-element.199) | copy-start | bytes 7077892
  173.4 15.9 %all-to-all-start.2 = ((f32[96,4,512]{2,0,1:T(8,128)}), f32[96,4,512]{2,0,1:T(8,128)}, u32[]{:S(2)}, u32[]{:S(2)}) async-start(f32[96,4,512]{2,0,1:T(8,128)} %copy.36), calls=%async_computation.2 | async-start | bytes 1572864 | tf_op jit(solution)/shard_map/all_to_all | solution.py:61
  193.5 24.1 %all-to-all-start.3 = ((f32[96,4,512]{2,0,1:T(8,128)}), f32[96,4,512]{2,0,1:T(8,128)}, u32[]{:S(2)}, u32[]{:S(2)}) async-start(f32[96,4,512]{2,0,1:T(8,128)} %bitcast.91), calls=%async_computation.3 | async-start | bytes 1572864 | tf_op jit(solution)/shard_map/all_to_all | solution.py:58
  353.5 15.1 %all-to-all-start.4 = ((f32[96,4,512]{2,0,1:T(8,128)}), f32[96,4,512]{2,0,1:T(8,128)S(1)}, u32[]{:S(2)}, u32[]{:S(2)}) async-start(f32[96,4,512]{2,0,1:T(8,128)} %copy.44), calls=%async_computation.4 | async-start | bytes 1572864 | tf_op jit(solution)/shard_map/all_to_all | solution.py:61
